TPU v7x, 128 devices: a whole 4x4x4 slice. The times are simulated.
128 devices in a mesh: cell: 128 (over z, x, y, core).
Axes of the slice: x: 4, y: 4, z: 4, core: 2. Of those that a mesh axis runs over, the one named last changes fastest.
Arguments:
- ocean_fields: float32 [12, 262144], P(None, 'cell'), may hold values from -6 to 6
- grad_coef: float32 [2, 4, 262144], P(None, None, 'cell'), may hold values from -4 to 4
- neighbors: int32 [4, 262144], P(None, 'cell'), may hold values from 0 to 262143, as said below
- task_source: int32 [12288], P('cell'), may hold values from 0 to 2047, as said below
- task_dest: int32 [12288], P('cell'), may hold values from 0 to 511, as said below
- area_weights: float32 [12288, 128, 128], P('cell'), may hold values from 0 to 0.015625
- moment_weights: float32 [12288, 2, 128, 128], P('cell'), may hold values from -0.046875 to 0.046875
Outputs:
- atmos_fields: float32 [12, 65536], P(None, 'cell')
Inputs may be any that keep to these rules, and one draw needn't show every extreme that they name: neighbors[k, c] lies within 128 cells of c. `task_source`: ocean block b lies on device b // 16; the 96 tasks of one device read blocks of 96 different devices. `task_dest`: atmosphere block g lies on device g // 4; a task held by device d has its destination either on a device at most 2 away from d (exactly 2 away for some tasks) or on device (d + 128 / 2) mod 128; every device holds some tasks of the latter kind.
All inputs are finite; a program needn't handle non-finite values.
Results may differ from a plain program's by a relative error of at most 0.000071.
Values sent between devices are 32-bit elements; how exact they have to be, the bound alone decides.
A program may use at most 64 MiB of HBM per device.

v0:
```python
import jax
import jax.numpy as jnp
from jax import lax
from jax.sharding import PartitionSpec as P

BLK = 128


def with_halo(cells, sides, width):
    for axis, dim in sides:
        count = lax.axis_size(axis)
        ends = count - 1
        head = lax.slice_in_dim(cells, 0, width, axis=dim)
        tail = lax.slice_in_dim(cells, cells.shape[dim] - width, cells.shape[dim], axis=dim)
        cells = jnp.concatenate(
            [
                lax.ppermute(tail, axis, [(i, (i + 1) % count) for i in range(ends)]),
                cells,
                lax.ppermute(head, axis, [((i + 1) % count, i) for i in range(ends)]),
            ],
            axis=dim,
        )
    return cells


def shards(
    ocean_fields, grad_coef, neighbors, task_source, task_dest, area_weights, moment_weights
):
    peer_count = lax.axis_size("cell")
    device_index = lax.axis_index("cell")
    field_count = ocean_fields.shape[0]
    cells_dev = ocean_fields.shape[1]
    src_blocks = cells_dev // BLK
    dst_blocks = cells_dev // (4 * BLK)
    widened = with_halo(ocean_fields, (("cell", 1),), BLK)
    shifted_idx = neighbors - (device_index * cells_dev - BLK)
    beside_all = jnp.take(widened, shifted_idx, axis=1)
    differ = beside_all - ocean_fields[:, None, :]
    slope_east = jnp.sum(grad_coef[0][None] * differ, axis=1)
    slope_north = jnp.sum(grad_coef[1][None] * differ, axis=1)
    rebuilt = jnp.stack([ocean_fields, slope_east, slope_north]).reshape(
        3, field_count, src_blocks, BLK
    )
    owner_dev = task_source // src_blocks
    within_dev = task_source % src_blocks
    peers = jnp.arange(peer_count, dtype=jnp.int32)
    wanted = jnp.sum(
        jnp.where(owner_dev[None, :] == peers[:, None], within_dev[None, :], 0), axis=1
    )
    requested = lax.all_to_all(wanted[:, None], "cell", split_axis=0, concat_axis=0, tiled=True)
    outgoing = jnp.take(rebuilt, requested[:, 0], axis=2)
    arrived = lax.all_to_all(outgoing, "cell", split_axis=2, concat_axis=2, tiled=True)
    picked = jnp.take(arrived, owner_dev, axis=2)
    partials = jnp.einsum("fti,tij->tfj", picked[0], area_weights, precision=lax.Precision.HIGHEST)
    partials = partials + jnp.einsum(
        "kfti,tkij->tfj", picked[1:], moment_weights, precision=lax.Precision.HIGHEST
    )
    targets = jnp.arange(dst_blocks * lax.axis_size("cell"), dtype=jnp.int32)
    selector = (task_dest[None, :] == targets[:, None]).astype(jnp.float32)
    collected = lax.psum_scatter(
        jnp.einsum("gt,tfj->gfj", selector, partials, precision=lax.Precision.HIGHEST),
        "cell",
        scatter_dimension=0,
        tiled=True,
    )
    return jnp.transpose(collected, (1, 0, 2)).reshape(field_count, dst_blocks * BLK)


def solution(mesh):
    placed = (
        P(None, "cell"),
        P(None, None, "cell"),
        P(None, "cell"),
        P("cell"),
        P("cell"),
        P("cell", None, None),
        P("cell", None, None, None),
    )
    return jax.shard_map(
        shards, mesh=mesh, in_specs=placed, out_specs=P(None, "cell"), check_vma=False
    )
```

profile of v0, /device:TPU:1, one launch (start us, length us, event | category | flops | bytes accessed | tf_op | source)
XLA Modules:
  0.0 305.4 jit_solution(5399881731803060356)
XLA Ops:
  6.5 0.7 fusion.13
  7.3 4.6 %collective-permute-start = (f32[12,128]{1,0:T(8,128)S(1)}, f32[12,128]{1,0:T(8,128)S(1)}, u32[]{:S(2)}, u32[]{:S(2)}) collective-permute-start(f32[12,128]{1,0:T(8,128)S(1)} %get-tuple-element.9), channel_id=1, source_target_pairs={{0,1},{1,2},{2,3},{3,4},{4,5},{5,6},{6,7},{7,8},{8,9},{9,10},{10,1... | collective-permute-start | bytes 18440 | tf_op jit(solution)/shard_map/ppermute | solution.py:17
  11.8 1.9 collective-permute-start.1
  13.8 0.7 compare_and_fusion.2
  14.4 0.7 and_select_fusion
  15.1 0.1 select_reduce_fusion
  15.2 0.7 copy.52
  15.9 10.5 %all-to-all-start = ((s32[128,1,1]{2,1,0:T(1,128)}), s32[128,1,1]{2,1,0:T(1,128)S(1)}, u32[]{:S(2)}, u32[]{:S(2)}) async-start(s32[128,1,1]{2,1,0:T(1,128)} %copy.52), calls=%async_computation | async-start | bytes 131072 | tf_op jit(solution)/shard_map/all_to_all | solution.py:50
  26.5 0.8 fusion.11
  27.3 0.8 compare_and_fusion
  28.1 0.8 slice_bitcast_fusion.3
  28.9 0.9 copy.70
  29.8 1.3 copy.54
  31.1 0.7 copy.57
  31.8 4.3 %all-to-all-done = s32[128,1,1]{2,1,0:T(1,128)S(1)} async-done(((s32[128,1,1]{2,1,0:T(1,128)}), s32[128,1,1]{2,1,0:T(1,128)S(1)}, u32[]{:S(2)}, u32[]{:S(2)}) %all-to-all-start) | async-done | bytes 544 | tf_op jit(solution)/shard_map/all_to_all | solution.py:50
  36.1 2.3 reduce
  38.5 0.0 collective-permute-done
  38.5 0.0 collective-permute-done.1
  38.5 0.9 pad_maximum_fusion.1
  39.4 0.4 copy.53
  39.8 27.8 %gather_fusion = f32[8192,12]{1,0:T(8,128)} fusion(f32[12,2304]{0,1:T(8,128)S(1)} %copy.53, s32[8192]{0:T(1024)S(1)} %broadcast_clamp_fusion), kind=kCustom, calls=%fused_computation | custom fusion | bytes 819200 | tf_op jit(solution)/shard_map/jit(_take)/gather | solution.py:37
  67.7 0.0 copy-start
  67.7 6.9 %multiply_reduce_fusion.1 = (f32[12,2048]{0,1:T(8,128)S(1)}, f32[12,2048]{0,1:T(8,128)S(1)}) fusion(f32[4,2048,12]{2,1,0:T(8,128)} %bitcast.47, f32[12,2048]{0,1:T(8,128)S(1)} %copy.54, f32[4,2048]{1,0:T(4,128)S(1)} %get-tuple-element.12, pred[4,2048]{1,0:T(4,128)(4,1)S(1)} %compare_and_fusion, f32[4,2048]{1,0:T(4,128)S(1)} %get-tuple-element.11), kind=kLoop, calls=%fused_computation.7 | loop fusion | flops 540672 | bytes 761856 | tf_op jit(solution)/shard_map/reduce_sum | solution.py:39
  74.5 0.3 copy.58
  74.9 0.3 copy.59
  75.2 0.0 copy-done
  75.3 0.8 gather_fusion.1
  76.0 1.9 select_bitcast_fusion
  77.9 5.4 %all-to-all-start.1 = ((f32[3,12,128,128]{3,1,0,2:T(8,128)}), f32[3,12,128,128]{3,1,0,2:T(8,128)S(1)}, u32[]{:S(2)}, u32[]{:S(2)}) async-start(f32[3,12,128,128]{3,1,0,2:T(8,128)} %select_bitcast_fusion), calls=%async_computation.1 | async-start | bytes 6291456 | tf_op jit(solution)/shard_map/all_to_all | solution.py:52
  83.4 0.2 all-reduce.3.cloned.1.call-start
  83.6 41.4 %all-to-all-done.1 = f32[3,12,128,128]{3,1,0,2:T(8,128)S(1)} async-done(((f32[3,12,128,128]{3,1,0,2:T(8,128)}), f32[3,12,128,128]{3,1,0,2:T(8,128)S(1)}, u32[]{:S(2)}, u32[]{:S(2)}) %all-to-all-start.1) | async-done | bytes 2359328 | tf_op jit(solution)/shard_map/all_to_all | solution.py:52
  125.0 1.9 copy.60
  127.0 2.6 gather_fusion.2
  129.6 0.0 slice-start
  129.6 0.2 fusion.2
  129.8 0.0 slice-start.1
  129.8 9.1 %fusion.3 = f32[96,12,128]{2,1,0:T(8,128)S(1)} fusion(f32[3,12,96,128]{3,1,2,0:T(8,128)S(1)} %fusion.2, f32[96,2,128,128]{3,2,1,0:T(8,128)} %param.13), kind=kOutput, calls=%fused_computation.11 | convolution fusion | flops 452984832 | bytes 14942208 | tf_op jit(solution)/shard_map/kfti,tkij->tfj/dot_general | solution.py:55
  138.9 0.0 slice-done
  138.9 0.0 slice-done.1
  138.9 0.0 copy-start.1
  138.9 5.6 %convolution_add_fusion = f32[96,12,128]{2,1,0:T(8,128)S(1)} fusion(f32[96,12,128]{2,1,0:T(8,128)S(1)} %fusion.3, f32[96,128,128]{2,1,0:T(8,128)S(1)} %bitcast.46, f32[3,12,96,128]{3,1,2,0:T(8,128)S(1)} %fusion.2), kind=kOutput, calls=%fused_computation.12 | convolution fusion | flops 226639872 | bytes 8454144 | tf_op jit(solution)/shard_map/fti,tij->tfj/dot_general | solution.py:54
  144.6 0.0 copy-done.1
  144.6 3.2 %fusion.6 = f32[512,12,128]{2,0,1:T(8,128)} fusion(f32[96,12,128]{2,1,0:T(8,128)S(1)} %convolution_add_fusion, s32[96]{0:T(128)S(1)} %copy-done.1), kind=kOutput, calls=%fused_computation.14 | convolution fusion | flops 906018816 | bytes 3735936 | tf_op jit(solution)/shard_map/gt,tfj->gfj/dot_general | solution.py:61
  147.8 0.0 all-reduce.3.cloned.1.call-update
  147.8 149.3 %all-reduce.3.cloned.1.call-done = f32[512,12,128]{2,0,1:T(8,128)} async-done(((f32[512,12,128]{2,0,1:T(8,128)}), f32[512,12,128]{2,0,1:T(8,128)}) %all-reduce.3.cloned.1.call-update) | async-done | bytes 3145744
  297.1 0.8 dynamic-slice_bitcast_fusion
  298.0 0.6 copy.72
  (11 shorter events, 0.1 us)
Async XLA Ops:
  7.3 31.2 %collective-permute-start = (f32[12,128]{1,0:T(8,128)S(1)}, f32[12,128]{1,0:T(8,128)S(1)}, u32[]{:S(2)}, u32[]{:S(2)}) collective-permute-start(f32[12,128]{1,0:T(8,128)S(1)} %get-tuple-element.9), channel_id=1, source_target_pairs={{0,1},{1,2},{2,3},{3,4},{4,5},{5,6},{6,7},{7,8},{8,9},{9,10},{10,1... | collective-permute-start | bytes 18440 | tf_op jit(solution)/shard_map/ppermute | solution.py:17
  11.8 26.7 %collective-permute-start.1 = (f32[12,128]{1,0:T(8,128)S(1)}, f32[12,128]{1,0:T(8,128)S(1)}, u32[]{:S(2)}, u32[]{:S(2)}) collective-permute-start(f32[12,128]{1,0:T(8,128)S(1)} %get-tuple-element.10), channel_id=1, source_target_pairs={{1,0},{2,1},{3,2},{4,3},{5,4},{6,5},{7,6},{8,7},{9,8},{10,9},{11,1... | collective-permute-start | bytes 18440 | tf_op jit(solution)/shard_map/ppermute | solution.py:19
  15.9 20.2 %all-to-all-start = ((s32[128,1,1]{2,1,0:T(1,128)}), s32[128,1,1]{2,1,0:T(1,128)S(1)}, u32[]{:S(2)}, u32[]{:S(2)}) async-start(s32[128,1,1]{2,1,0:T(1,128)} %copy.52), calls=%async_computation | async-start | bytes 131072 | tf_op jit(solution)/shard_map/all_to_all | solution.py:50
  67.7 7.5 %copy-start = (f32[1,12,16,128]{3,1,2,0:T(8,128)S(1)}, f32[1,12,16,128]{3,1,2,0:T(8,128)}, u32[]{:S(2)}) copy-start(f32[1,12,16,128]{3,1,2,0:T(8,128)} %copy.57) | copy-start | bytes 294916
  77.9 47.1 %all-to-all-start.1 = ((f32[3,12,128,128]{3,1,0,2:T(8,128)}), f32[3,12,128,128]{3,1,0,2:T(8,128)S(1)}, u32[]{:S(2)}, u32[]{:S(2)}) async-start(f32[3,12,128,128]{3,1,0,2:T(8,128)} %select_bitcast_fusion), calls=%async_computation.1 | async-start | bytes 6291456 | tf_op jit(solution)/shard_map/all_to_all | solution.py:52
  83.4 213.8 %all-reduce.3.cloned.1.call-start = ((), (), s32[]{:S(2)}) async-start(), calls=%async_computation.2 | async-start | bytes 6291456
  129.6 9.4 %slice-start = ((s8[6291456]{0:T(1024)(128)(4,1)}), s8[4194304]{0:T(1024)(128)(4,1)S(1)}, s32[]{:S(2)}) async-start(s8[6291456]{0:T(1024)(128)(4,1)} %bitcast.45), calls=%async_computation.3 | async-start | bytes 8388608
  129.8 9.1 %slice-start.1 = ((s8[6291456]{0:T(1024)(128)(4,1)}), s8[2097152]{0:T(1024)(128)(4,1)S(1)}, s32[]{:S(2)}) async-start(s8[6291456]{0:T(1024)(128)(4,1)} %bitcast.45), calls=%async_computation.4 | async-start | bytes 4194304
  138.9 5.6 %copy-start.1 = (s32[96]{0:T(128)S(1)}, s32[96]{0:T(128)}, u32[]{:S(2)}) copy-start(s32[96]{0:T(128)} %param.11) | copy-start | bytes 1156
Sparse Core Ops, SparseCore 0:
  147.9 149.1 all-reduce.2
where the time goes:
time: 306 us; the launch traced here: 305 us
  waiting for transfers between devices  195 us (64%)
  local copies, waits for them, and re-layouts  40.7 us (13%)
  starting transfers between devices  22.7 us (7%)
  matrix products  17.9 us (6%)
  other arithmetic  15.4 us (5%)
  between operations  13.7 us (4%)
    unnamed x2, waiting for transfers between devices  149 us
    all_to_all x1, waiting for transfers between devices, shards(): lax.all_to_all(outgoing, 'cell', split_axis=2, concat_axis=2, tiled=True)  41.4 us
    gather x1, local copies, waits for them, and re-layouts, shards(): beside_all = jnp.take(widened, shifted_idx, axis=1)  27.8 us
    all_to_all x1, starting transfers between devices, shards(): lax.all_to_all(wanted[:, None], 'cell', split_axis=0, concat_axis=0, tile...  10.5 us
    dot_general x1, matrix products, shards(): jnp.einsum('kfti,tkij->tfj', picked[1:], moment_weights, precision=lax.Pr...  9.08 us
    reduce_sum x1, other arithmetic, shards(): slope_east = jnp.sum(grad_coef[0][None] * differ, axis=1)  6.85 us
  transfers between devices with their start and end apart: 5, of which 3 were waited for; matrix products, arithmetic and copies ran while one was open for 3% of the time, Pallas kernels for 0%

commit v1 on v0

v1 whole, which is shorter than its diff:
```python
import jax
import jax.numpy as jnp
from jax import lax
from jax.experimental import pallas as pl
from jax.experimental.pallas import tpu as pltpu
from jax.sharding import PartitionSpec as P

MESH = pl.DeviceIdType.MESH
BLK = 128
ROWS = 16
AXES = 3
SIDE = 4
STRIDES = (32, 8, 2)
SPREAD = 11
NEAR = (-2, -1, 1, 2)
WEIGHT_CHUNKS = 4


def slot_offset(axis, slot):
    first, second, core = slot // 8, (slot // 2) % 4, slot % 2
    offset = [first, second]
    offset.insert(axis, 0)
    return (*offset, core)


def negated(offset):
    return (*((-step) % SIDE for step in offset[:3]), offset[3])


PEERS = []
for _slot in range(1, 32):
    for _axis in range(AXES):
        if slot_offset(_axis, _slot) not in PEERS:
            PEERS.append(slot_offset(_axis, _slot))
PEER_ROW = {offset: row for row, offset in enumerate(PEERS)}
PEER_ROW[(0, 0, 0, 0)] = len(PEERS)
WANT_ROWS = len(PEERS)
WANT_PAD = (WANT_ROWS + 8) // 8 * 8


def kernel(
    ocean,
    coef,
    near_cells,
    source,
    dest,
    area,
    moment,
    out,
    window,
    gather_0,
    gather_1,
    gather_2,
    want,
    own_table,
    mask,
    outgoing,
    arrived,
    total,
    final,
    area_v,
    moment_v,
    want_s,
    own_s,
    weight_sem,
    table_sem,
    want_sems,
    halo_sems,
    spread_send,
    spread_recv,
    block_send,
    block_recv,
    final_send,
    final_recv,
):
    gathers = (gather_0, gather_1, gather_2)
    fields, cells = ocean.shape
    blocks = cells // BLK
    tasks = source.shape[0]
    devices = lax.axis_size("cell")
    me = lax.axis_index("cell")
    place = [(me // stride) % SIDE for stride in STRIDES]
    core = me % 2
    along = [
        [((place[axis] + step) % SIDE) * STRIDES[axis] for step in range(SIDE)] for axis in range(AXES)
    ]
    cores = [core, 1 - core]

    def device_at(offset):
        return along[0][offset[0]] + along[1][offset[1]] + along[2][offset[2]] + cores[offset[3]]

    def index_at(distance):
        return (me + distance + devices) % devices

    weight_copies = []
    step = tasks // WEIGHT_CHUNKS
    for chunk in range(WEIGHT_CHUNKS):
        part = pl.ds(chunk * step, step)
        weight_copies.append(
            pltpu.make_async_copy(area.at[part], area_v.at[part], weight_sem.at[2 * chunk])
        )
        weight_copies.append(
            pltpu.make_async_copy(moment.at[part], moment_v.at[part], weight_sem.at[2 * chunk + 1])
        )
    for copy in weight_copies:
        copy.start()

    barrier = pltpu.get_barrier_semaphore()
    for offset in PEERS:
        pl.semaphore_signal(barrier, inc=1, device_id=(device_at(offset),), device_id_type=MESH)
    for distance in NEAR:
        pl.semaphore_signal(barrier, inc=1, device_id=(index_at(distance),), device_id_type=MESH)

    lanes = lax.broadcasted_iota(jnp.int32, (8, BLK), 1)

    def note(task, tables):
        wanted, reader, slot = tables
        origin = source[task]
        goal = dest[task]
        here = lanes == origin // blocks
        away = (goal // SIDE - me + 2 + devices) % devices
        away = jnp.where(away > 4, 5, away)
        return (
            jnp.where(here, origin % blocks, wanted),
            jnp.where(here, task, reader),
            jnp.where(here, away * SIDE + goal % SIDE, slot),
        )

    empty = jnp.zeros((8, BLK), jnp.int32)
    wanted, reader, slot = lax.fori_loop(0, tasks, note, (empty, empty, empty - 1))
    want[pl.ds(WANT_ROWS, 1), :] = wanted[0:1]
    own_table[0:1, :] = reader[0:1]
    own_table[1:2, :] = slot[0:1]
    table_copy = pltpu.make_async_copy(own_table, own_s, table_sem.at[0])
    table_copy.start()

    for block in range(blocks):
        piece = ocean[:, block * BLK : (block + 1) * BLK]
        window[block + 1, 0:fields, :] = piece
        gather_0[0, block, 0:fields, :] = piece

    def slopes(block):
        first_cell = me * cells + (block - 1) * BLK
        column = pl.ds(pl.multiple_of(block * BLK, BLK), BLK)
        for rows in (slice(0, 8), slice(8, ROWS)):
            left = window[block, rows, :]
            mid = window[block + 1, rows, :]
            right = window[block + 2, rows, :]
            east = jnp.zeros_like(mid)
            north = jnp.zeros_like(mid)
            for k in range(4):
                at = jnp.broadcast_to(near_cells[k : k + 1, column], mid.shape) - first_cell
                lane = at & (BLK - 1)
                which = at >> 7
                picks = [
                    jnp.take_along_axis(x, lane, axis=1, mode="promise_in_bounds")
                    for x in (left, mid, right)
                ]
                beside = jnp.where(which == 0, picks[0], jnp.where(which == 1, picks[1], picks[2]))
                differ = beside - mid
                east += jnp.broadcast_to(coef[0, k : k + 1, column], mid.shape) * differ
                north += jnp.broadcast_to(coef[1, k : k + 1, column], mid.shape) * differ
            gather_1[0, block, rows, :] = east
            gather_2[0, block, rows, :] = north

    def inner(block, carry):
        slopes(block)
        return carry

    lax.fori_loop(1, blocks - 1, inner, 0)

    table_copy.wait()
    slots = lax.broadcasted_iota(jnp.int32, (24, BLK), 0)

    def mark(p, carry):
        mask[p] = jnp.where(slots == own_s[1, p], 1.0, 0.0)
        return carry

    lax.fori_loop(0, devices, mark, 0)
    total[...] = jnp.zeros_like(total)

    pl.semaphore_wait(barrier, len(PEERS) + len(NEAR))

    real = pl.ds(0, fields)
    to_right = pltpu.make_async_remote_copy(
        window.at[blocks, real], window.at[0, real], halo_sems.at[0], halo_sems.at[1],
        device_id=(index_at(1),), device_id_type=MESH,
    )
    to_left = pltpu.make_async_remote_copy(
        window.at[1, real], window.at[blocks + 1, real], halo_sems.at[2], halo_sems.at[3],
        device_id=(index_at(-1),), device_id_type=MESH,
    )
    to_right.start()
    to_left.start()
    for offset in PEERS:
        pltpu.make_async_remote_copy(
            want.at[pl.ds(WANT_ROWS, 1)], want.at[pl.ds(PEER_ROW[offset], 1)], want_sems.at[0], want_sems.at[1],
            device_id=(device_at(offset),), device_id_type=MESH,
        ).start()

    def spread(axis):
        copies = []
        for step in (2, 1, 3):
            offset = [0, 0, 0, 0]
            offset[axis] = step
            copies.append(
                pltpu.make_async_remote_copy(
                    gathers[axis].at[0, :, real], gathers[axis].at[step, :, real],
                    spread_send.at[axis, step], spread_recv.at[axis, step],
                    device_id=(device_at(offset),), device_id_type=MESH,
                )
            )
        return copies

    spreads = [spread(axis) for axis in range(AXES)]
    for copy in spreads[0]:
        copy.start()

    to_right.wait_recv()
    to_left.wait_recv()
    slopes(0)
    slopes(blocks - 1)
    for one, other in zip(spreads[1], spreads[2]):
        one.start()
        other.start()

    all_wants = pl.ds(0, WANT_ROWS)
    pltpu.make_async_copy(want.at[all_wants], want.at[all_wants], want_sems.at[1]).wait()
    want_copy = pltpu.make_async_copy(want, want_s, table_sem.at[1])
    want_copy.start()
    want_copy.wait()

    columns = [
        [me - along[axis][0] + along[axis][(-step) % SIDE] for step in range(SIDE)] for axis in range(AXES)
    ]

    def fill(axis, slot):
        row = PEER_ROW[slot_offset(axis, slot)]
        for step in range(SIDE):
            block = want_s[row, columns[axis][step]]
            piece = gathers[axis][step, block]
            if slot == 0:
                arrived[axis, 0, step] = piece
            else:
                outgoing[axis, slot, step] = piece

    def send(axis, slot):
        return pltpu.make_async_remote_copy(
            outgoing.at[axis, slot, :, real], arrived.at[axis, slot, :, real],
            block_send.at[0], block_recv.at[axis, slot],
            device_id=(device_at(negated(slot_offset(axis, slot))),), device_id_type=MESH,
        )

    for axis in range(AXES):
        for copy in spreads[axis]:
            copy.wait_recv()
    before = []
    for order in range(1, 32):
        slot = (SPREAD * order) % 32
        for axis in range(AXES):
            fill(axis, slot)
        for axis, earlier in before:
            send(axis, earlier).start()
        before = [(axis, slot) for axis in range(AXES)]
    for axis in range(AXES):
        fill(axis, 0)
    for axis, earlier in before:
        send(axis, earlier).start()

    for copy in weight_copies:
        copy.wait()

    def split(x):
        high = x.astype(jnp.bfloat16)
        low = (x - high.astype(jnp.float32)).astype(jnp.bfloat16)
        return high, low

    def products(slot):
        first, second, side = slot // 8, (slot // 2) % 4, slot % 2
        partials = []
        owners = []
        for axis in range(AXES):
            steps = [first, second]
            steps.insert(axis, 0)
            for step in range(SIDE):
                steps[axis] = step
                owner = (core + side) % 2
                for a in range(AXES):
                    shift = -steps[a] if a == axis else steps[a]
                    owner = owner + ((place[a] + shift + SIDE) % SIDE) * STRIDES[a]
                task = own_s[0, owner]
                weight = area_v[task] if axis == 0 else moment_v[task, axis - 1]
                weight = jnp.concatenate(split(weight), axis=1)
                value = jnp.concatenate(split(arrived[axis, slot, step]), axis=0)
                product = jnp.dot(value, weight, preferred_element_type=jnp.float32)
                partials.append(
                    (product[:ROWS, :BLK] + product[ROWS:, :BLK])
                    + (product[:ROWS, BLK:] + product[ROWS:, BLK:])
                )
                owners.append(owner)
        for goal in range(24):
            added = total[goal]
            for owner, partial in zip(owners, partials):
                added += jnp.broadcast_to(mask[owner, goal : goal + 1, :], (ROWS, BLK)) * partial
            total[goal] = added

    products(0)

    def body(order, carry):
        slot = (SPREAD * order) % 32
        for axis in range(AXES):
            pltpu.make_async_copy(
                arrived.at[axis, slot, :, real], arrived.at[axis, slot, :, real], block_recv.at[axis, slot]
            ).wait()
        products(slot)
        return carry

    lax.fori_loop(1, 32, body, 0)

    goals = [index_at(distance) for distance in NEAR] + [index_at(devices // 2)]
    origins = (0, 1, 3, 4, 5)
    finals = [
        pltpu.make_async_remote_copy(
            total.at[pl.ds(SIDE * away, SIDE), real], final.at[number, :, real],
            final_send.at[number], final_recv.at[number],
            device_id=(goal,), device_id_type=MESH,
        )
        for number, (away, goal) in enumerate(zip(origins, goals))
    ]
    for copy in reversed(finals):
        copy.start()
    for copy in finals:
        copy.wait_recv()
    for block in range(SIDE):
        added = total[2 * SIDE + block, 0:fields]
        for number in range(len(finals)):
            added += final[number, block, 0:fields]
        out[:, block * BLK : (block + 1) * BLK] = added

    to_right.wait_send()
    to_left.wait_send()
    pltpu.make_async_copy(want.at[all_wants], want.at[all_wants], want_sems.at[0]).wait()
    for copies in spreads:
        for copy in copies:
            copy.wait_send()
    sent = outgoing.at[:, pl.ds(1, 31), :, real]
    pltpu.make_async_copy(sent, sent, block_send.at[0]).wait()
    for copy in finals:
        copy.wait_send()


def shards(ocean_fields, grad_coef, neighbors, task_source, task_dest, area_weights, moment_weights):
    fields, cells = ocean_fields.shape
    tasks = task_source.shape[0]
    blocks = cells // BLK
    devices = lax.axis_size("cell")
    f32, i32 = jnp.float32, jnp.int32
    vmem = pl.BlockSpec(memory_space=pltpu.VMEM)
    smem = pl.BlockSpec(memory_space=pltpu.SMEM)
    far = pl.BlockSpec(memory_space=pl.ANY)
    dma = pltpu.SemaphoreType.DMA
    gather = pltpu.VMEM((SIDE, blocks, ROWS, BLK), f32)
    return pl.pallas_call(
        kernel,
        out_shape=jax.ShapeDtypeStruct((fields, cells // SIDE), f32),
        in_specs=[vmem, vmem, vmem, smem, smem, far, far],
        out_specs=vmem,
        scratch_shapes=[
            pltpu.VMEM((blocks + 2, ROWS, BLK), f32),
            gather,
            gather,
            gather,
            pltpu.VMEM((WANT_PAD, BLK), i32),
            pltpu.VMEM((8, BLK), i32),
            pltpu.VMEM((devices, 24, BLK), f32),
            pltpu.VMEM((AXES, 32, SIDE, ROWS, BLK), f32),
            pltpu.VMEM((AXES, 32, SIDE, ROWS, BLK), f32),
            pltpu.VMEM((24, ROWS, BLK), f32),
            pltpu.VMEM((5, SIDE, ROWS, BLK), f32),
            pltpu.VMEM((tasks, BLK, BLK), f32),
            pltpu.VMEM((tasks, 2, BLK, BLK), f32),
            pltpu.SMEM((WANT_PAD, BLK), i32),
            pltpu.SMEM((8, BLK), i32),
            dma((2 * WEIGHT_CHUNKS,)),
            dma((2,)),
            dma((2,)),
            dma((4,)),
            dma((AXES, SIDE)),
            dma((AXES, SIDE)),
            dma((1,)),
            dma((AXES, 32)),
            dma((5,)),
            dma((5,)),
        ],
        compiler_params=pltpu.CompilerParams(
            collective_id=0, has_side_effects=True, vmem_limit_bytes=60 << 20
        ),
    )(ocean_fields, grad_coef, neighbors, task_source, task_dest, area_weights, moment_weights)


def solution(mesh):
    placed = (
        P(None, "cell"),
        P(None, None, "cell"),
        P(None, "cell"),
        P("cell"),
        P("cell"),
        P("cell", None, None),
        P("cell", None, None, None),
    )
    return jax.shard_map(
        shards, mesh=mesh, in_specs=placed, out_specs=P(None, "cell"), check_vma=False
    )
```

time: 306 us -> 51.5 us (0.17)
  waiting for transfers between devices: 195 us -> 0 us
  Pallas kernels: 0 us -> 49.2 us
  local copies, waits for them, and re-layouts: 40.7 us -> 1.38 us
  starting transfers between devices: 22.7 us -> 0 us
  matrix products: 17.9 us -> 0 us
  other arithmetic: 15.4 us -> 0 us
  between operations: 13.7 us -> 0.01 us
    unnamed x2 -> x0, waiting for transfers between devices: 149 us -> none
    pallas_call x0 -> x1, Pallas kernels: none -> 49.2 us  [shards(): pl.pallas_call(kernel, out_shape=jax.ShapeDtypeStruct((fields, cells // S...]
    all_to_all x2 -> x0, waiting for transfers between devices: 45.7 us -> none  [the longest x1 41.4 us: shards(): lax.all_to_all(outgoing, 'cell', split_axis=2, concat_axis=2, tiled=True)]
    gather x3 -> x0, local copies, waits for them, and re-layouts: 31.2 us -> none  [the longest x1 27.8 us: shards(): beside_all = jnp.take(widened, shifted_idx, axis=1)]
    dot_general x3 -> x0, matrix products: 17.9 us -> none  [the longest x1 9.08 us: shards(): jnp.einsum('kfti,tkij->tfj', picked[1:], moment_weights, precision=lax.Pr...]
    all_to_all x2 -> x0, starting transfers between devices: 16 us -> none  [the longest x1 10.5 us: shards(): lax.all_to_all(wanted[:, None], 'cell', split_axis=0, concat_axis=0, tile...]
    reduce_sum x2 -> x0, other arithmetic: 6.96 us -> none  [the longest x1 6.85 us: shards(): slope_east = jnp.sum(grad_coef[0][None] * differ, axis=1)]
    ppermute x2 -> x0, starting transfers between devices: 6.49 us -> none  [the longest x1 4.57 us: with_halo(): lax.ppermute(tail, axis, [(i, (i + 1) % count) for i in range(ends)])]
  transfers between devices with their start and end apart: 5 -> 0, of which waited for: 3 -> 0; matrix products, arithmetic and copies ran while one was open for 3% -> 0% of each run, Pallas kernels for 0% -> 0%
where the time goes in v1:
time: 51.5 us; the launch traced here: 50.6 us
  Pallas kernels  49.2 us (96%)
  local copies, waits for them, and re-layouts  1.38 us (3%)
    pallas_call x1, Pallas kernels, shards(): pl.pallas_call(kernel, out_shape=jax.ShapeDtypeStruct((fields, cells // S...  49.2 us
    unnamed x1, local copies, waits for them, and re-layouts  1.38 us

profile of v1, /device:TPU:1, one launch (start us, length us, event | category | flops | bytes accessed | tf_op | source)
XLA Modules:
  0.0 50.6 jit_solution(14471249913630875855)
XLA Ops:
  0.0 49.2 %shard_map.73 = f32[12,512]{1,0:T(8,128)} custom-call(f32[12,2048]{1,0:T(8,128)} %ocean.1, f32[2,4,2048]{2,1,0:T(4,128)} %coef.1, s32[4,2048]{1,0:T(4,128)} %near_cells.1, s32[96]{0:T(128)} %source.1, s32[96]{0:T(128)} %dest.1, f32[96,128,128]{2,1,0:T(8,128)} %area.1, f32[96,2,128,128]{3,2,1,0:T(8,128)} %moment.1), custom_call_target="tpu_custom_call" | custom-call | tf_op jit(solution)/shard_map/pallas_call | solution.py:363
  49.2 1.4 %copy.9 = f32[12,512]{1,0:T(8,128)} copy(f32[12,512]{1,0:T(8,128)} %shard_map.73) | data formatting | bytes 49152

commit v2 on v1

--- a/solution.py
+++ b/solution.py
@@ -18,8 +18,9 @@
 
 def slot_offset(axis, slot):
     first, second, core = slot // 8, (slot // 2) % 4, slot % 2
-    offset = [first, second]
-    offset.insert(axis, 0)
+    offset = [0, 0, 0]
+    offset[(axis + 1) % AXES] = first
+    offset[(axis + 2) % AXES] = second
     return (*offset, core)
 
 
@@ -39,18 +40,24 @@
 
 
 def kernel(
-    ocean,
-    coef,
-    near_cells,
+    ocean_far,
+    coef_far,
+    near_far,
     source,
     dest,
     area,
     moment,
     out,
+    ocean,
+    coef,
+    near_cells,
     window,
-    gather_0,
-    gather_1,
-    gather_2,
+    own_0,
+    own_1,
+    own_2,
+    line_0,
+    line_1,
+    line_2,
     want,
     own_table,
     mask,
@@ -62,18 +69,21 @@
     moment_v,
     want_s,
     own_s,
+    input_sem,
     weight_sem,
     table_sem,
     want_sems,
     halo_sems,
     spread_send,
     spread_recv,
+    edge_send,
+    edge_recv,
     block_send,
     block_recv,
     final_send,
     final_recv,
 ):
-    gathers = (gather_0, gather_1, gather_2)
+    owns, lines = (own_0, own_1, own_2), (line_0, line_1, line_2)
     fields, cells = ocean.shape
     blocks = cells // BLK
     tasks = source.shape[0]
@@ -92,6 +102,26 @@
     def index_at(distance):
         return (me + distance + devices) % devices
 
+    barrier = pltpu.get_barrier_semaphore()
+    for offset in PEERS:
+        pl.semaphore_signal(barrier, inc=1, device_id=(device_at(offset),), device_id_type=MESH)
+    has_left, has_right = me > 0, me < devices - 1
+    corner_left = jnp.logical_and(has_left, me % STRIDES[0] == 0)
+    corner_right = jnp.logical_and(has_right, me % STRIDES[0] == STRIDES[0] - 1)
+
+    @pl.when(corner_left)
+    def _():
+        pl.semaphore_signal(barrier, inc=1, device_id=(index_at(-1),), device_id_type=MESH)
+
+    @pl.when(corner_right)
+    def _():
+        pl.semaphore_signal(barrier, inc=1, device_id=(index_at(1),), device_id_type=MESH)
+
+    input_copies = [
+        pltpu.make_async_copy(ocean_far, ocean, input_sem.at[0]),
+        pltpu.make_async_copy(near_far, near_cells, input_sem.at[1]),
+        pltpu.make_async_copy(coef_far, coef, input_sem.at[2]),
+    ]
     weight_copies = []
     step = tasks // WEIGHT_CHUNKS
     for chunk in range(WEIGHT_CHUNKS):
@@ -102,14 +132,8 @@
         weight_copies.append(
             pltpu.make_async_copy(moment.at[part], moment_v.at[part], weight_sem.at[2 * chunk + 1])
         )
-    for copy in weight_copies:
+    for copy in input_copies:
         copy.start()
-
-    barrier = pltpu.get_barrier_semaphore()
-    for offset in PEERS:
-        pl.semaphore_signal(barrier, inc=1, device_id=(device_at(offset),), device_id_type=MESH)
-    for distance in NEAR:
-        pl.semaphore_signal(barrier, inc=1, device_id=(index_at(distance),), device_id_type=MESH)
 
     lanes = lax.broadcasted_iota(jnp.int32, (8, BLK), 1)
 
@@ -117,27 +141,31 @@
         wanted, reader, slot = tables
         origin = source[task]
         goal = dest[task]
-        here = lanes == origin // blocks
-        away = (goal // SIDE - me + 2 + devices) % devices
-        away = jnp.where(away > 4, 5, away)
+        here = lanes == origin >> 4
+        away = ((goal >> 2) - me + 2 + devices) & (devices - 1)
+        away = jnp.minimum(away, 5)
         return (
-            jnp.where(here, origin % blocks, wanted),
+            jnp.where(here, origin & 15, wanted),
             jnp.where(here, task, reader),
-            jnp.where(here, away * SIDE + goal % SIDE, slot),
+            jnp.where(here, away * SIDE + (goal & 3), slot),
         )
 
     empty = jnp.zeros((8, BLK), jnp.int32)
-    wanted, reader, slot = lax.fori_loop(0, tasks, note, (empty, empty, empty - 1))
+    wanted, reader, slot = lax.fori_loop(0, tasks, note, (empty, empty, empty - 1), unroll=8)
     want[pl.ds(WANT_ROWS, 1), :] = wanted[0:1]
     own_table[0:1, :] = reader[0:1]
     own_table[1:2, :] = slot[0:1]
     table_copy = pltpu.make_async_copy(own_table, own_s, table_sem.at[0])
     table_copy.start()
 
+    for copy in input_copies:
+        copy.wait()
+    for copy in weight_copies:
+        copy.start()
     for block in range(blocks):
         piece = ocean[:, block * BLK : (block + 1) * BLK]
         window[block + 1, 0:fields, :] = piece
-        gather_0[0, block, 0:fields, :] = piece
+        own_0[block, 0:fields, :] = piece
 
     def slopes(block):
         first_cell = me * cells + (block - 1) * BLK
@@ -160,28 +188,39 @@
                 differ = beside - mid
                 east += jnp.broadcast_to(coef[0, k : k + 1, column], mid.shape) * differ
                 north += jnp.broadcast_to(coef[1, k : k + 1, column], mid.shape) * differ
-            gather_1[0, block, rows, :] = east
-            gather_2[0, block, rows, :] = north
+            own_1[block, rows, :] = east
+            own_2[block, rows, :] = north
 
     def inner(block, carry):
         slopes(block)
         return carry
 
-    lax.fori_loop(1, blocks - 1, inner, 0)
-
-    table_copy.wait()
-    slots = lax.broadcasted_iota(jnp.int32, (24, BLK), 0)
-
-    def mark(p, carry):
-        mask[p] = jnp.where(slots == own_s[1, p], 1.0, 0.0)
-        return carry
-
-    lax.fori_loop(0, devices, mark, 0)
-    total[...] = jnp.zeros_like(total)
-
-    pl.semaphore_wait(barrier, len(PEERS) + len(NEAR))
+    lax.fori_loop(1, blocks - 1, inner, 0, unroll=2)
 
     real = pl.ds(0, fields)
+
+    def spread(axis, part, send_sem, recv_sem):
+        copies = []
+        for step in (2, 1, 3):
+            offset = [0, 0, 0, 0]
+            offset[axis] = step
+            copies.append(
+                pltpu.make_async_remote_copy(
+                    owns[axis].at[part, real], lines[axis].at[step - 1, part, real],
+                    send_sem.at[axis, step], recv_sem.at[axis, step],
+                    device_id=(device_at(offset),), device_id_type=MESH,
+                )
+            )
+        return copies
+
+    inside = pl.ds(1, blocks - 2)
+    spreads = [spread(0, pl.ds(0, blocks), spread_send, spread_recv)] + [
+        spread(axis, inside, spread_send, spread_recv) for axis in (1, 2)
+    ]
+
+    corners = corner_left.astype(jnp.int32) + corner_right.astype(jnp.int32)
+    pl.semaphore_wait(barrier, len(PEERS) + corners)
+
     to_right = pltpu.make_async_remote_copy(
         window.at[blocks, real], window.at[0, real], halo_sems.at[0], halo_sems.at[1],
         device_id=(index_at(1),), device_id_type=MESH,
@@ -190,39 +229,43 @@
         window.at[1, real], window.at[blocks + 1, real], halo_sems.at[2], halo_sems.at[3],
         device_id=(index_at(-1),), device_id_type=MESH,
     )
-    to_right.start()
-    to_left.start()
+    pl.when(has_right)(to_right.start)
+    pl.when(has_left)(to_left.start)
     for offset in PEERS:
         pltpu.make_async_remote_copy(
             want.at[pl.ds(WANT_ROWS, 1)], want.at[pl.ds(PEER_ROW[offset], 1)], want_sems.at[0], want_sems.at[1],
             device_id=(device_at(offset),), device_id_type=MESH,
         ).start()
 
-    def spread(axis):
-        copies = []
-        for step in (2, 1, 3):
-            offset = [0, 0, 0, 0]
-            offset[axis] = step
-            copies.append(
-                pltpu.make_async_remote_copy(
-                    gathers[axis].at[0, :, real], gathers[axis].at[step, :, real],
-                    spread_send.at[axis, step], spread_recv.at[axis, step],
-                    device_id=(device_at(offset),), device_id_type=MESH,
-                )
-            )
-        return copies
-
-    spreads = [spread(axis) for axis in range(AXES)]
-    for copy in spreads[0]:
-        copy.start()
-
-    to_right.wait_recv()
-    to_left.wait_recv()
+    for copies in list(zip(*spreads))[1:]:
+        for copy in copies:
+            copy.start()
+
+    table_copy.wait()
+    slots = lax.broadcasted_iota(jnp.int32, (24, BLK), 0)
+
+    def mark(p, carry):
+        mask[p] = jnp.where(slots == own_s[1, p], 1.0, 0.0)
+        return carry
+
+    lax.fori_loop(0, devices, mark, 0, unroll=8)
+    total[...] = jnp.zeros_like(total)
+
+    pl.when(has_left)(to_right.wait_recv)
+    pl.when(has_right)(to_left.wait_recv)
     slopes(0)
     slopes(blocks - 1)
-    for one, other in zip(spreads[1], spreads[2]):
-        one.start()
-        other.start()
+    edges = [
+        copy
+        for side, block in enumerate((0, blocks - 1))
+        for axis in (1, 2)
+        for copy in spread(axis, pl.ds(block, 1), edge_send.at[side], edge_recv.at[side])
+    ]
+    for copy in edges:
+        copy.start()
+
+    for copy in next(zip(*spreads)):
+        copy.start()
 
     all_wants = pl.ds(0, WANT_ROWS)
     pltpu.make_async_copy(want.at[all_wants], want.at[all_wants], want_sems.at[1]).wait()
@@ -234,38 +277,42 @@
         [me - along[axis][0] + along[axis][(-step) % SIDE] for step in range(SIDE)] for axis in range(AXES)
     ]
 
-    def fill(axis, slot):
+    def fill(axis, slot, steps):
         row = PEER_ROW[slot_offset(axis, slot)]
-        for step in range(SIDE):
+        for step in steps:
             block = want_s[row, columns[axis][step]]
-            piece = gathers[axis][step, block]
+            piece = lines[axis][step - 1, block] if step else owns[axis][block]
             if slot == 0:
                 arrived[axis, 0, step] = piece
             else:
                 outgoing[axis, slot, step] = piece
 
-    def send(axis, slot):
+    def send(axis, slot, steps):
+        part = pl.ds(steps.start, len(steps))
         return pltpu.make_async_remote_copy(
-            outgoing.at[axis, slot, :, real], arrived.at[axis, slot, :, real],
+            outgoing.at[axis, slot, part, real], arrived.at[axis, slot, part, real],
             block_send.at[0], block_recv.at[axis, slot],
             device_id=(device_at(negated(slot_offset(axis, slot))),), device_id_type=MESH,
         )
 
-    for axis in range(AXES):
-        for copy in spreads[axis]:
-            copy.wait_recv()
-    before = []
-    for order in range(1, 32):
-        slot = (SPREAD * order) % 32
+    def serve(steps):
+        before = []
+        for order in range(1, 32):
+            slot = (SPREAD * order) % 32
+            for axis in range(AXES):
+                fill(axis, slot, steps)
+            for axis, earlier in before:
+                send(axis, earlier, steps).start()
+            before = [(axis, slot) for axis in range(AXES)]
         for axis in range(AXES):
-            fill(axis, slot)
+            fill(axis, 0, steps)
         for axis, earlier in before:
-            send(axis, earlier).start()
-        before = [(axis, slot) for axis in range(AXES)]
-    for axis in range(AXES):
-        fill(axis, 0)
-    for axis, earlier in before:
-        send(axis, earlier).start()
+            send(axis, earlier, steps).start()
+
+    serve(range(1))
+    for copy in sum(spreads, edges):
+        copy.wait_recv()
+    serve(range(1, SIDE))
 
     for copy in weight_copies:
         copy.wait()
@@ -280,10 +327,10 @@
         partials = []
         owners = []
         for axis in range(AXES):
-            steps = [first, second]
-            steps.insert(axis, 0)
             for step in range(SIDE):
-                steps[axis] = step
+                steps = [step] * AXES
+                steps[(axis + 1) % AXES] = first
+                steps[(axis + 2) % AXES] = second
                 owner = (core + side) % 2
                 for a in range(AXES):
                     shift = -steps[a] if a == axis else steps[a]
@@ -337,12 +384,11 @@
             added += final[number, block, 0:fields]
         out[:, block * BLK : (block + 1) * BLK] = added
 
-    to_right.wait_send()
-    to_left.wait_send()
+    pl.when(has_right)(to_right.wait_send)
+    pl.when(has_left)(to_left.wait_send)
     pltpu.make_async_copy(want.at[all_wants], want.at[all_wants], want_sems.at[0]).wait()
-    for copies in spreads:
-        for copy in copies:
-            copy.wait_send()
+    for copy in sum(spreads, edges):
+        copy.wait_send()
     sent = outgoing.at[:, pl.ds(1, 31), :, real]
     pltpu.make_async_copy(sent, sent, block_send.at[0]).wait()
     for copy in finals:
@@ -359,17 +405,24 @@
     smem = pl.BlockSpec(memory_space=pltpu.SMEM)
     far = pl.BlockSpec(memory_space=pl.ANY)
     dma = pltpu.SemaphoreType.DMA
-    gather = pltpu.VMEM((SIDE, blocks, ROWS, BLK), f32)
+    own = pltpu.VMEM((blocks, ROWS, BLK), f32)
+    line = pltpu.VMEM((SIDE - 1, blocks, ROWS, BLK), f32)
     return pl.pallas_call(
         kernel,
-        out_shape=jax.ShapeDtypeStruct((fields, cells // SIDE), f32),
-        in_specs=[vmem, vmem, vmem, smem, smem, far, far],
+        out_shape=pltpu.VMEM((fields, cells // SIDE), f32),
+        in_specs=[far, far, far, smem, smem, far, far],
         out_specs=vmem,
         scratch_shapes=[
+            pltpu.VMEM(ocean_fields.shape, f32),
+            pltpu.VMEM(grad_coef.shape, f32),
+            pltpu.VMEM(neighbors.shape, i32),
             pltpu.VMEM((blocks + 2, ROWS, BLK), f32),
-            gather,
-            gather,
-            gather,
+            own,
+            own,
+            own,
+            line,
+            line,
+            line,
             pltpu.VMEM((WANT_PAD, BLK), i32),
             pltpu.VMEM((8, BLK), i32),
             pltpu.VMEM((devices, 24, BLK), f32),
@@ -381,12 +434,15 @@
             pltpu.VMEM((tasks, 2, BLK, BLK), f32),
             pltpu.SMEM((WANT_PAD, BLK), i32),
             pltpu.SMEM((8, BLK), i32),
+            dma((3,)),
             dma((2 * WEIGHT_CHUNKS,)),
             dma((2,)),
             dma((2,)),
             dma((4,)),
             dma((AXES, SIDE)),
             dma((AXES, SIDE)),
+            dma((2, AXES, SIDE)),
+            dma((2, AXES, SIDE)),
             dma((1,)),
             dma((AXES, 32)),
             dma((5,)),

time: 51.5 us -> 45 us (0.87); the launches traced: 50.6 us -> 44.8 us
  Pallas kernels: 49.2 us -> 44.2 us
  local copies, waits for them, and re-layouts: 1.38 us -> 0.62 us
    pallas_call x1, Pallas kernels: 49.2 us -> 44.2 us  [shards(): pl.pallas_call(kernel, out_shape=pltpu.VMEM((fields, cells // SIDE), f32)...]
    unnamed x1, local copies, waits for them, and re-layouts: 1.38 us -> 0.62 us
where the time goes in v2:
time: 45 us; the launch traced here: 44.8 us
  Pallas kernels  44.2 us (98%)
  local copies, waits for them, and re-layouts  0.62 us (1%)
    pallas_call x1, Pallas kernels, shards(): pl.pallas_call(kernel, out_shape=pltpu.VMEM((fields, cells // SIDE), f32)...  44.2 us

profile of v2, /device:TPU:1, one launch (start us, length us, event | category | flops | bytes accessed | tf_op | source)
XLA Modules:
  0.0 44.8 jit_solution(13492463936118608039)
XLA Ops:
  0.0 44.2 %shard_map.73 = f32[12,512]{1,0:T(8,128)S(1)} custom-call(f32[12,2048]{1,0:T(8,128)} %ocean_far.1, f32[2,4,2048]{2,1,0:T(4,128)} %coef_far.1, s32[4,2048]{1,0:T(4,128)} %near_far.1, s32[96]{0:T(128)} %source.1, s32[96]{0:T(128)} %dest.1, f32[96,128,128]{2,1,0:T(8,128)} %area.1, f32[96,2,128,128]{3,2,1,0:T(8,128)} %moment.1), custom_call_target="tpu_custom_call" | custom-call | tf_op jit(solution)/shard_map/pallas_call | solution.py:410
  44.2 0.6 %copy.9 = f32[12,512]{1,0:T(8,128)} copy(f32[12,512]{1,0:T(8,128)S(1)} %shard_map.73) | data formatting | bytes 49152
